TPU v7x, 512 devices: a whole 4x8x8 slice. The times are simulated.
512 devices in a mesh: sample: 32 (over y, x), space: 16 (over z, core).
Axes of the slice: x: 4, y: 8, z: 8, core: 2. Of those that a mesh axis runs over, the one named last changes fastest.
Arguments:
- input_field: bfloat16 [32, 64, 64, 4, 128], P('sample', None, 'space'), may hold values from -6 to 6
- out_cotangent: bfloat16 [32, 256, 16, 1, 32], P('sample', None, 'space'), may hold values from -6 to 6
- first_weight: bfloat16 [27, 64, 128], replicated, may hold values from -0.15625 to 0.15625
- second_weight: bfloat16 [27, 128, 256], replicated, may hold values from -0.109375 to 0.109375
Outputs:
- input_grad: bfloat16 [32, 64, 64, 4, 128], P('sample', None, 'space')
- first_grad: bfloat16 [27, 64, 128], replicated
- second_grad: bfloat16 [27, 128, 256], P(None, None, 'space')
All inputs are finite; a program needn't handle non-finite values.
Results may differ from a plain program's by a relative error of at most 0.008.
Values may be sent and summed in bfloat16 or wider, within the bound.
No kernel may reach another device: no remote copies, remote signals or barrier semaphores. Data moves between devices by JAX's collectives and lax.ppermute only.
A program may use at most 64 MiB of HBM per device.

v0:
```python
import math
import jax
import jax.numpy as jnp
from jax import lax
from jax.sharding import PartitionSpec as P


def shifted(value, axis, steps):
    count = lax.axis_size(axis)
    initial, last = (max(0, -steps), min(count, count - steps))
    return lax.ppermute(value, axis, [(source, source + steps) for source in range(initial, last)])


def gradient_silu(values):
    logistic = jax.nn.sigmoid(values)
    return logistic * (1.0 + values * (1.0 - logistic))


def parity_split(padded, extents):
    planes_n, rows_n, cells_n = extents
    channels = padded.shape[0]
    grid = jnp.pad(padded, ((0, 0), (0, 1), (0, 1), (0, 1)))
    grid = grid.reshape(channels, planes_n + 1, 2, rows_n + 1, 2, cells_n + 1, 2)
    return grid.transpose(2, 4, 6, 0, 1, 3, 5)


def tap_block(split, extents, offset):
    planes_n, rows_n, cells_n = extents
    slices = []
    for row_tap in range(3):
        for cell_tap in range(3):
            piece = split[offset % 2, row_tap % 2, cell_tap % 2]
            slices.append(
                piece[
                    :,
                    offset // 2 : offset // 2 + planes_n,
                    row_tap // 2 : row_tap // 2 + rows_n,
                    cell_tap // 2 : cell_tap // 2 + cells_n,
                ]
            )
    stacked = jnp.stack(slices, 0)
    return stacked.reshape(-1, planes_n * rows_n * cells_n)


def make_blocks(padded, extents):
    split = parity_split(padded, extents)
    return [tap_block(split, extents, offset) for offset in range(3)]


def apply_filters(blocks, weight):
    channels = weight.shape[1]
    grouped = weight.reshape(3, 9 * channels, weight.shape[2])
    summed = lax.dot_general(
        grouped[0], blocks[0], (((0,), (0,)), ((), ())), preferred_element_type=jnp.float32
    )
    for offset in (1, 2):
        summed = summed + lax.dot_general(
            grouped[offset],
            blocks[offset],
            (((0,), (0,)), ((), ())),
            preferred_element_type=jnp.float32,
        )
    return summed


def filter_gradient(blocks, deltas):
    products = [
        lax.dot_general(
            tap_rows, deltas, (((1,), (1,)), ((), ())), preferred_element_type=jnp.float32
        )
        for tap_rows in blocks
    ]
    stacked = jnp.stack(products, 0)
    return stacked.reshape(27, -1, deltas.shape[0])


def alternate(taps, spatial):
    leading, central, trailing = (taps[0], taps[1], taps[2])
    planes_in = central.shape[spatial]
    widths = [(0, 0)] * leading.ndim
    upper_pad = list(widths)
    upper_pad[spatial] = (0, 1)
    lower_pad = list(widths)
    lower_pad[spatial] = (1, 0)
    even_part = jnp.pad(leading, upper_pad) + jnp.pad(trailing, lower_pad)
    paired = jnp.stack(
        [lax.slice_in_dim(even_part, 0, planes_in, axis=spatial), central], spatial + 1
    )
    target = list(central.shape)
    target[spatial] = 2 * planes_in
    merged = paired.reshape(target)
    return jnp.concatenate(
        [merged, lax.slice_in_dim(even_part, planes_in, planes_in + 1, axis=spatial)], spatial
    )


def spread_back(weight, deltas, extents):
    channels, filters = (weight.shape[1], weight.shape[2])
    flat_weight = weight.reshape(27 * channels, filters)
    patches = jnp.dot(flat_weight, deltas, preferred_element_type=jnp.float32)
    spread = patches.reshape((3, 3, 3, channels) + tuple(extents))
    spread = alternate(spread, 3)
    spread = alternate(spread, 3)
    spread = alternate(spread, 3)
    return spread


def shards(input_field, out_cotangent, first_weight, second_weight):
    volume = input_field[0]
    chan_in, planes, height, length = volume.shape
    chan_mid = first_weight.shape[2]
    chan_out = second_weight.shape[2]
    groups = lax.axis_size("space")
    samples_n = lax.axis_size("sample")
    first_ext = (planes // 2, height // 2, length // 2)
    second_ext = (planes // 4, height // 4, length // 4)
    lower_rim = shifted(volume[:, planes - 1 :], "space", 1)
    padded = jnp.pad(jnp.concatenate([lower_rim, volume], 1), ((0, 0), (0, 0), (1, 0), (1, 0)))
    first_blocks = make_blocks(padded, first_ext)
    first_pre = apply_filters(first_blocks, first_weight)
    hidden = jax.nn.silu(first_pre).astype(jnp.bfloat16).reshape((chan_mid,) + first_ext)
    cotangent = out_cotangent[0]
    gathered = lax.all_gather(hidden, "space", axis=1, tiled=True)
    gathered_pad = jnp.pad(gathered, ((0, 0), (1, 0), (1, 0), (1, 0)))
    gathered_ext = (gathered.shape[1] // 2, height // 4, length // 4)
    gathered_blocks = make_blocks(gathered_pad, gathered_ext)
    per_group = chan_out // groups
    own_weight = lax.dynamic_slice_in_dim(
        second_weight, lax.axis_index("space") * per_group, per_group, 2
    )
    own_pre = apply_filters(gathered_blocks, own_weight)
    own_cotangent = lax.all_to_all(
        cotangent, "space", split_axis=0, concat_axis=1, tiled=True
    ).reshape(per_group, -1)
    own_delta = (own_cotangent.astype(jnp.float32) * gradient_silu(own_pre)).astype(jnp.bfloat16)
    second_part = filter_gradient(gathered_blocks, own_delta)
    second_delta = lax.all_to_all(
        own_delta.reshape((per_group,) + gathered_ext),
        "space",
        split_axis=1,
        concat_axis=0,
        tiled=True,
    ).reshape(chan_out, -1)
    second_total = lax.psum(second_part, "sample")
    grad_pad = spread_back(second_weight, second_delta, second_ext)
    returned = shifted(grad_pad[:, :1, 1:, 1:], "space", -1)
    interior = grad_pad[:, 1:, 1:, 1:]
    hidden_grad = jnp.concatenate([interior[:, :-1], interior[:, -1:] + returned], 1)
    first_delta = (hidden_grad.reshape(chan_mid, -1) * gradient_silu(first_pre)).astype(
        jnp.bfloat16
    )
    first_part = filter_gradient(first_blocks, first_delta)
    first_total = lax.psum(first_part, ("sample", "space"))
    input_pad = spread_back(first_weight, first_delta, first_ext)
    input_back = shifted(input_pad[:, :1, 1:, 1:].astype(jnp.bfloat16), "space", -1).astype(
        jnp.float32
    )
    input_inner = input_pad[:, 1:, 1:, 1:]
    volume_grad = jnp.concatenate([input_inner[:, :-1], input_inner[:, -1:] + input_back], 1)
    first_scale = 1.0 / math.sqrt(samples_n * groups * first_ext[0] * first_ext[1] * first_ext[2])
    second_scale = 1.0 / math.sqrt(
        samples_n * groups * second_ext[0] * second_ext[1] * second_ext[2]
    )
    input_grad = volume_grad.astype(jnp.bfloat16)[None]
    return (
        input_grad,
        (first_total * first_scale).astype(jnp.bfloat16),
        (second_total * second_scale).astype(jnp.bfloat16),
    )


def solution(mesh):
    placed = (
        P("sample", None, "space", None, None),
        P("sample", None, "space", None, None),
        P(),
        P(),
    )
    return jax.shard_map(
        shards,
        mesh=mesh,
        in_specs=placed,
        out_specs=(P("sample", None, "space", None, None), P(), P(None, None, "space")),
        check_vma=False,
    )
```

profile of v0, /device:TPU:1, one launch (start us, length us, event | category | flops | bytes accessed | tf_op | source)
XLA Modules:
  0.0 558.1 jit_solution(18105045833384356062)
XLA Ops:
  7.2 0.9 slice.510
  8.1 5.4 collective-permute-start
  13.5 1.8 fusion.69
  15.3 1.7 collective-permute-done
  17.9 1.6 reshape.138
  19.6 2.4 fusion.67
  22.0 1.1 copy.637
  24.9 0.7 constant_dynamic-update-slice_fusion.24
  27.0 0.8 constant_dynamic-update-slice_fusion.21
  29.0 0.7 constant_dynamic-update-slice_fusion.18
  29.7 1.7 copy.641
  35.6 1.0 multiply_convert_fusion.2
  37.9 0.7 reshape.162
  38.6 9.7 %all-to-all-start = ((bf16[16,2,256]{2,1,0:T(2,128)(2,1)}), bf16[16,2,256]{2,1,0:T(2,128)(2,1)S(1)}, u32[]{:S(2)}, u32[]{:S(2)}) async-start(bf16[16,2,256]{2,1,0:T(2,128)(2,1)} %reshape.162), calls=%async_computation | async-start | bytes 32768 | tf_op jit(solution)/shard_map/all_to_all | solution.py:132
  48.3 1.0 constant_dynamic-slice_fusion.1
  49.4 6.3 %all-to-all-done = bf16[16,2,256]{2,1,0:T(2,128)(2,1)S(1)} async-done(((bf16[16,2,256]{2,1,0:T(2,128)(2,1)}), bf16[16,2,256]{2,1,0:T(2,128)(2,1)S(1)}, u32[]{:S(2)}, u32[]{:S(2)}) %all-to-all-start) | async-done | bytes 16416 | tf_op jit(solution)/shard_map/all_to_all | solution.py:132
  56.0 26.5 %all-gather.2.cloned.1.call-done = bf16[128,32,2,64]{0,3,2,1:T(8,128)(2,1)} async-done(((bf16[128,2,2,64]{0,3,2,1:T(8,128)(2,1)}), bf16[128,32,2,64]{0,3,2,1:T(8,128)(2,1)}) %all-gather.2.cloned.1.call-update) | async-done | bytes 1048592 | tf_op jit(solution)/shard_map/all_gather | solution.py:123
  82.5 2.3 copy.719
  84.8 1.4 pad.117
  86.2 3.2 fusion.65
  90.6 2.3 fusion.70
  94.5 0.9 copy.654
  96.4 0.9 fusion.74
  98.0 0.9 copy.658
  99.3 0.9 copy.659
  102.4 0.7 reshape.164
  103.1 4.5 all-to-all-start.1
  107.9 7.0 %all-to-all-done.1 = bf16[16,2,256]{2,1,0:T(2,128)(2,1)S(1)} async-done(((bf16[16,2,256]{2,1,0:T(2,128)(2,1)}), bf16[16,2,256]{2,1,0:T(2,128)(2,1)S(1)}, u32[]{:S(2)}, u32[]{:S(2)}) %all-to-all-start.1) | async-done | bytes 16416 | tf_op jit(solution)/shard_map/all_to_all | solution.py:137
  115.0 2.1 convolution_bitcast_fusion
  118.6 2.3 collective-permute-start.1
  121.1 0.8 reshape.159
  122.2 1.9 collective-permute-done.1
  124.3 1.0 convolution_bitcast_fusion.6
  125.3 1.0 convolution_bitcast_fusion.5
  126.7 0.7 squeeze.176
  127.6 0.7 squeeze.177
  128.7 0.7 stack_squeeze.21
  131.9 1.4 pad_add_fusion
  133.5 2.4 copy.673
  135.9 1.4 copy.674
  137.7 1.9 collective-permute-start.2
  139.9 1.0 pad_maximum_fusion.5
  140.9 3.5 collective-permute-done.2
  144.5 1.0 copy.676
  145.5 124.9 %all-reduce.21.cloned.1.call-done = f32[27,128,16]{1,0,2:T(8,128)} async-done(((f32[27,128,16]{1,0,2:T(8,128)}), f32[27,128,16]{1,0,2:T(8,128)}) %all-reduce.21.cloned.1.call-update) | async-done | bytes 221200 | tf_op jit(solution)/shard_map/psum | solution.py:144
  270.4 1.0 multiply_convert_fusion.1
  272.1 277.4 %all-reduce.19.cloned.1.call-done = f32[27,64,128]{2,1,0:T(8,128)} async-done(((f32[27,64,128]{2,1,0:T(8,128)}), f32[27,64,128]{2,1,0:T(8,128)}) %all-reduce.19.cloned.1.call-update) | async-done | bytes 884752 | tf_op jit(solution)/shard_map/psum | solution.py:153
  549.5 2.1 multiply_convert_fusion
  (163 shorter events, 25.1 us)
Async XLA Ops:
  7.2 9.9 %copy-start.11 = (bf16[1,64,4,4,128]{4,3,2,1,0:T(4,128)(2,1)S(1)}, bf16[1,64,4,4,128]{4,3,2,1,0:T(4,128)(2,1)}, u32[]{:S(2)}) copy-start(bf16[1,64,4,4,128]{4,3,2,1,0:T(4,128)(2,1)} %param.4) | copy-start | bytes 786436
  7.2 75.3 %all-gather.2.cloned.1.call-start = ((), (), s32[]{:S(2)}) async-start(), calls=%async_computation.2 | async-start | bytes 1114112 | tf_op jit(solution)/shard_map/all_gather | solution.py:123
  8.1 8.9 %collective-permute-start = (bf16[64,1,4,128]{3,2,1,0:T(4,128)(2,1)S(1)}, bf16[64,1,4,128]{3,2,1,0:T(4,128)(2,1)S(1)}, u32[]{:S(2)}, u32[]{:S(2)}) collective-permute-start(bf16[64,1,4,128]{3,2,1,0:T(4,128)(2,1)S(1)} %slice.510), channel_id=1, source_target_pairs={{0,1},{1,2},{2,3},{3,4},{4,5},{5,6},{6,7},{7,8},{8,9},{9,10},{10,1... | collective-permute-start | bytes 196616 | tf_op jit(solution)/shard_map/ppermute | solution.py:11
  31.8 3.2 copy-start.1
  33.9 1.0 copy-start.9
  33.9 1.4 copy-start.10
  34.6 1.1 copy-start.12
  35.0 2.2 copy-start.13
  35.0 13.3 %copy-start = (bf16[27,128,256]{2,1,0:T(8,128)(2,1)S(1)}, bf16[27,128,256]{2,1,0:T(8,128)(2,1)}, u32[]{:S(2)}) copy-start(bf16[27,128,256]{2,1,0:T(8,128)(2,1)} %param.7) | copy-start | bytes 5308420
  38.6 17.0 %all-to-all-start = ((bf16[16,2,256]{2,1,0:T(2,128)(2,1)}), bf16[16,2,256]{2,1,0:T(2,128)(2,1)S(1)}, u32[]{:S(2)}, u32[]{:S(2)}) async-start(bf16[16,2,256]{2,1,0:T(2,128)(2,1)} %reshape.162), calls=%async_computation | async-start | bytes 32768 | tf_op jit(solution)/shard_map/all_to_all | solution.py:132
  99.3 1.0 copy-start.8
  103.1 11.8 %all-to-all-start.1 = ((bf16[16,2,256]{2,1,0:T(2,128)(2,1)}), bf16[16,2,256]{2,1,0:T(2,128)(2,1)S(1)}, u32[]{:S(2)}, u32[]{:S(2)}) async-start(bf16[16,2,256]{2,1,0:T(2,128)(2,1)} %reshape.164), calls=%async_computation.1 | async-start | bytes 32768 | tf_op jit(solution)/shard_map/all_to_all | solution.py:137
  107.5 162.8 %all-reduce.21.cloned.1.call-start = ((), (), s32[]{:S(2)}) async-start(), calls=%async_computation.4 | async-start | bytes 524288 | tf_op jit(solution)/shard_map/psum | solution.py:144
  118.6 5.6 %collective-permute-start.1 = (f32[128,1,2,64]{0,3,2,1:T(8,128)S(1)}, f32[128,1,2,64]{0,3,2,1:T(8,128)S(1)}, u32[]{:S(2)}, u32[]{:S(2)}) collective-permute-start(f32[128,1,2,64]{0,3,2,1:T(8,128)S(1)} %pad_maximum_fusion.15), channel_id=1, source_target_pairs={{1,0},{2,1},{3,2},{4,3},{5,4},{6,5},{7,6},{8,7},{9,8},{10,9},{11,1... | collective-permute-start | bytes 196616 | tf_op jit(solution)/shard_map/ppermute | solution.py:11
  121.9 4.3 copy-start.3
  121.9 427.5 %all-reduce.19.cloned.1.call-start = ((), (), s32[]{:S(2)}) async-start(), calls=%async_computation.3 | async-start | bytes 1769472 | tf_op jit(solution)/shard_map/psum | solution.py:153
  124.3 2.3 copy-start.4
  137.3 2.3 copy-start.2
  137.3 2.3 copy-start.5
  137.5 2.4 copy-start.6
  137.5 2.4 copy-start.7
  137.7 6.7 %collective-permute-start.2 = (bf16[64,1,4,128]{0,3,2,1:T(8,128)(2,1)S(1)}, bf16[64,1,4,128]{0,3,2,1:T(8,128)(2,1)S(1)}, u32[]{:S(2)}, u32[]{:S(2)}) collective-permute-start(bf16[64,1,4,128]{0,3,2,1:T(8,128)(2,1)S(1)} %slice.614), channel_id=1, source_target_pairs={{1,0},{2,1},{3,2},{4,3},{5,4},{6,5},{7,6},{8,7},{9,8},{10,9},{11,1... | collective-permute-start | bytes 196616 | tf_op jit(solution)/shard_map/ppermute | solution.py:11
Sparse Core Ops, SparseCore 0:
  36.7 45.7 all-gather.1
  122.0 148.2 all-reduce.20
  275.4 274.0 all-reduce.18
where the time goes:
time: 559 us; the launch traced here: 558 us
  waiting for transfers between devices  449 us (80%)
  local copies, waits for them, and re-layouts  51.6 us (9%)
  starting transfers between devices  24.1 us (4%)
  between operations  14.8 us (3%)
  other arithmetic  9.86 us (2%)
  matrix products  8.46 us (2%)
    psum x1, waiting for transfers between devices, shards(): first_total = lax.psum(first_part, ('sample', 'space'))  277 us
    psum x1, waiting for transfers between devices, shards(): second_total = lax.psum(second_part, 'sample')  125 us
    all_gather x1, waiting for transfers between devices, shards(): gathered = lax.all_gather(hidden, 'space', axis=1, tiled=True)  26.5 us
    unnamed x80, local copies, waits for them, and re-layouts  13.9 us
  transfers between devices with their start and end apart: 8, of which 8 were waited for; matrix products, arithmetic and copies ran while one was open for 4% of the time, Pallas kernels for 0%

commit v1 on v0

--- a/solution.py
+++ b/solution.py
@@ -141,7 +141,7 @@
         concat_axis=0,
         tiled=True,
     ).reshape(chan_out, -1)
-    second_total = lax.psum(second_part, "sample")
+    second_total = jnp.sum(lax.all_gather(second_part, "sample"), axis=0)
     grad_pad = spread_back(second_weight, second_delta, second_ext)
     returned = shifted(grad_pad[:, :1, 1:, 1:], "space", -1)
     interior = grad_pad[:, 1:, 1:, 1:]

time: 559 us -> 508 us (0.909)
  waiting for transfers between devices: 449 us -> 370 us
  local copies, waits for them, and re-layouts: 51.6 us -> 66.4 us
  blocking collectives: 0 us -> 11.6 us
  other arithmetic: 9.86 us -> 15.7 us
    psum x1 -> x0, waiting for transfers between devices: 125 us -> none  [shards(): second_total = lax.psum(second_part, 'sample')]
    all_gather x0 -> x1, waiting for transfers between devices: none -> 94.2 us  [shards(): second_total = jnp.sum(lax.all_gather(second_part, 'sample'), axis=0)]
    psum x1, waiting for transfers between devices: 277 us -> 234 us  [shards(): first_total = lax.psum(first_part, ('sample', 'space'))]
    all_to_all x0 -> x1, blocking collectives: none -> 11.6 us  [shards(): lax.all_to_all(own_delta.reshape((per_group,) + gathered_ext), 'space', s...]
    all_to_all x1 -> x0, waiting for transfers between devices: 6.96 us -> none  [shards(): lax.all_to_all(own_delta.reshape((per_group,) + gathered_ext), 'space', s...]
    unnamed x80 -> x84, local copies, waits for them, and re-layouts: 13.9 us -> 16.3 us
  transfers between devices with their start and end apart: 8 -> 7, of which waited for: 8 -> 7; matrix products, arithmetic and copies ran while one was open for 4% -> 7% of each run, Pallas kernels for 0% -> 0%
where the time goes in v1:
time: 508 us; the launch traced here: 507 us
  waiting for transfers between devices  370 us (73%)
  local copies, waits for them, and re-layouts  66.4 us (13%)
  starting transfers between devices  19.6 us (4%)
  other arithmetic  15.7 us (3%)
  between operations  14.8 us (3%)
  blocking collectives  11.6 us (2%)
  matrix products  8.62 us (2%)
    psum x1, waiting for transfers between devices, shards(): first_total = lax.psum(first_part, ('sample', 'space'))  234 us
    all_gather x1, waiting for transfers between devices, shards(): second_total = jnp.sum(lax.all_gather(second_part, 'sample'), axis=0)  94.2 us
    all_gather x1, waiting for transfers between devices, shards(): gathered = lax.all_gather(hidden, 'space', axis=1, tiled=True)  26.5 us
    unnamed x84, local copies, waits for them, and re-layouts  16.3 us
    all_to_all x1, blocking collectives, shards(): lax.all_to_all(own_delta.reshape((per_group,) + gathered_ext), 'space', s...  11.6 us
  transfers between devices with their start and end apart: 7, of which 7 were waited for; matrix products, arithmetic and copies ran while one was open for 7% of the time, Pallas kernels for 0%

profile of v1, /device:TPU:1, one launch (start us, length us, event | category | flops | bytes accessed | tf_op | source)
XLA Modules:
  0.0 506.7 jit_solution(1931657952110758818)
XLA Ops:
  7.2 0.9 slice.510
  8.1 5.4 %collective-permute-start = (bf16[64,1,4,128]{3,2,1,0:T(4,128)(2,1)S(1)}, bf16[64,1,4,128]{3,2,1,0:T(4,128)(2,1)S(1)}, u32[]{:S(2)}, u32[]{:S(2)}) collective-permute-start(bf16[64,1,4,128]{3,2,1,0:T(4,128)(2,1)S(1)} %slice.510), channel_id=1, source_target_pairs={{0,1},{1,2},{2,3},{3,4},{4,5},{5,6},{6,7},{7,8},{8,9},{9,10},{10,1... | collective-permute-start | bytes 196616 | tf_op jit(solution)/shard_map/ppermute | solution.py:11
  13.5 1.8 fusion.70
  15.3 1.7 collective-permute-done
  17.9 1.6 reshape.135
  19.6 2.5 fusion.68
  22.1 1.2 copy.629
  23.9 1.1 copy.630
  30.8 1.7 copy.633
  36.7 1.0 multiply_convert_fusion.1
  39.7 9.7 %all-to-all-start = ((bf16[16,2,256]{2,1,0:T(2,128)(2,1)}), bf16[16,2,256]{2,1,0:T(2,128)(2,1)S(1)}, u32[]{:S(2)}, u32[]{:S(2)}) async-start(bf16[16,2,256]{2,1,0:T(2,128)(2,1)} %reshape.158), calls=%async_computation | async-start | bytes 32768 | tf_op jit(solution)/shard_map/all_to_all | solution.py:132
  49.4 1.2 constant_dynamic-slice_fusion.1
  50.6 6.1 %all-to-all-done = bf16[16,2,256]{2,1,0:T(2,128)(2,1)S(1)} async-done(((bf16[16,2,256]{2,1,0:T(2,128)(2,1)}), bf16[16,2,256]{2,1,0:T(2,128)(2,1)S(1)}, u32[]{:S(2)}, u32[]{:S(2)}) %all-to-all-start) | async-done | bytes 16416 | tf_op jit(solution)/shard_map/all_to_all | solution.py:132
  57.0 26.5 %all-gather.3.cloned.1.call-done = bf16[128,32,2,64]{0,3,2,1:T(8,128)(2,1)} async-done(((bf16[128,2,2,64]{0,3,2,1:T(8,128)(2,1)}), bf16[128,32,2,64]{0,3,2,1:T(8,128)(2,1)}) %all-gather.3.cloned.1.call-update) | async-done | bytes 1048592 | tf_op jit(solution)/shard_map/all_gather | solution.py:123
  83.5 2.3 copy.714
  85.8 1.4 pad.117
  87.2 3.4 fusion.66
  91.9 1.9 fusion.71
  95.6 0.9 copy.646
  99.1 0.9 copy.650
  100.3 0.9 copy.651
  103.6 11.6 %all_to_all.24 = bf16[16,2,256]{2,1,0:T(2,128)(2,1)S(1)} all-to-all(bf16[16,2,256]{2,1,0:T(2,128)(2,1)S(1)} %reshape.160), channel_id=1, replica_groups=mesh['sample'=32,'space'=16] {'space'}, dimensions={0} | all-to-all | bytes 32768 | tf_op jit(solution)/shard_map/all_to_all | solution.py:137
  115.3 2.1 convolution_bitcast_fusion
  118.2 1.0 squeeze.171
  119.2 1.6 stack_squeeze.18
  120.9 1.0 maximum_bitcast_fusion
  123.0 2.4 collective-permute-start.1
  125.8 2.9 collective-permute-done.1
  129.6 1.0 pad_maximum_fusion.5
  131.8 1.9 convolution_bitcast_fusion.2
  135.2 1.3 fusion.67
  136.5 1.8 squeeze.176
  138.5 0.9 copy-done.6
  139.3 1.8 squeeze.177
  141.2 1.5 copy.661
  142.7 1.8 stack_squeeze.21
  144.5 1.4 copy.662
  148.8 1.5 pad_maximum_fusion.3
  150.3 3.4 copy.665
  153.6 2.6 pad_add_fusion
  156.3 1.4 copy.666
  157.9 1.9 collective-permute-start.2
  160.0 4.7 collective-permute-done.2
  164.9 1.0 copy.670
  165.8 233.8 %all-reduce.18.cloned.1.call-done = f32[27,64,128]{2,1,0:T(8,128)} async-done(((f32[27,64,128]{2,1,0:T(8,128)}), f32[27,64,128]{2,1,0:T(8,128)}) %all-reduce.18.cloned.1.call-update) | async-done | bytes 884752 | tf_op jit(solution)/shard_map/psum | solution.py:153
  399.6 2.1 multiply_convert_fusion
  401.7 94.2 %all-gather.5.cloned.1.call-done = f32[32,27,128,16]{2,3,1,0:T(8,128)} async-done(((f32[1,27,128,16]{2,3,1,0:T(8,128)}), f32[32,27,128,16]{2,3,1,0:T(8,128)}) %all-gather.5.cloned.1.call-update) | async-done | bytes 7077904 | tf_op jit(solution)/shard_map/all_gather | solution.py:144
  495.9 3.5 reduce_sum.9
  (168 shorter events, 31.8 us)
Async XLA Ops:
  7.2 9.9 %copy-start.12 = (bf16[1,64,4,4,128]{4,3,2,1,0:T(4,128)(2,1)S(1)}, bf16[1,64,4,4,128]{4,3,2,1,0:T(4,128)(2,1)}, u32[]{:S(2)}) copy-start(bf16[1,64,4,4,128]{4,3,2,1,0:T(4,128)(2,1)} %param.4) | copy-start | bytes 786436
  7.2 76.4 %all-gather.3.cloned.1.call-start = ((), (), s32[]{:S(2)}) async-start(), calls=%async_computation.2 | async-start | bytes 1114112 | tf_op jit(solution)/shard_map/all_gather | solution.py:123
  8.1 8.9 %collective-permute-start = (bf16[64,1,4,128]{3,2,1,0:T(4,128)(2,1)S(1)}, bf16[64,1,4,128]{3,2,1,0:T(4,128)(2,1)S(1)}, u32[]{:S(2)}, u32[]{:S(2)}) collective-permute-start(bf16[64,1,4,128]{3,2,1,0:T(4,128)(2,1)S(1)} %slice.510), channel_id=1, source_target_pairs={{0,1},{1,2},{2,3},{3,4},{4,5},{5,6},{6,7},{7,8},{8,9},{9,10},{10,1... | collective-permute-start | bytes 196616 | tf_op jit(solution)/shard_map/ppermute | solution.py:11
  22.1 2.9 copy-start.8
  35.0 1.4 copy-start.11
  35.6 1.0 copy-start.13
  36.0 2.2 copy-start.15
  36.0 13.4 %copy-start.4 = (bf16[27,128,256]{2,1,0:T(8,128)(2,1)S(1)}, bf16[27,128,256]{2,1,0:T(8,128)(2,1)}, u32[]{:S(2)}) copy-start(bf16[27,128,256]{2,1,0:T(8,128)(2,1)} %param.7) | copy-start | bytes 5308420
  39.7 17.0 %all-to-all-start = ((bf16[16,2,256]{2,1,0:T(2,128)(2,1)}), bf16[16,2,256]{2,1,0:T(2,128)(2,1)S(1)}, u32[]{:S(2)}, u32[]{:S(2)}) async-start(bf16[16,2,256]{2,1,0:T(2,128)(2,1)} %reshape.158), calls=%async_computation | async-start | bytes 32768 | tf_op jit(solution)/shard_map/all_to_all | solution.py:132
  49.4 350.3 %all-reduce.18.cloned.1.call-start = ((), (), s32[]{:S(2)}) async-start(), calls=%async_computation.3 | async-start | bytes 1769472 | tf_op jit(solution)/shard_map/psum | solution.py:153
  100.0 1.4 copy-start
  100.3 1.2 copy-start.10
  101.3 1.6 copy-start.2
  101.3 1.2 copy-start.9
  123.0 5.8 %copy-start.14 = (f32[128,256]{0,1:T(8,128)S(1)}, f32[128,256]{0,1:T(8,128)}, u32[]{:S(2)}) copy-start(f32[128,256]{0,1:T(8,128)} %get-tuple-element.128) | copy-start | bytes 393220
  123.0 5.7 %collective-permute-start.1 = (f32[128,1,2,64]{0,3,2,1:T(8,128)S(1)}, f32[128,1,2,64]{0,3,2,1:T(8,128)S(1)}, u32[]{:S(2)}, u32[]{:S(2)}) collective-permute-start(f32[128,1,2,64]{0,3,2,1:T(8,128)S(1)} %pad_maximum_fusion.15), channel_id=1, source_target_pairs={{1,0},{2,1},{3,2},{4,3},{5,4},{6,5},{7,6},{8,7},{9,8},{10,9},{11,1... | collective-permute-start | bytes 196616 | tf_op jit(solution)/shard_map/ppermute | solution.py:11
  129.6 1.9 copy-start.1
  130.6 365.3 %all-gather.5.cloned.1.call-start = ((), (), s32[]{:S(2)}) async-start(), calls=%async_computation.4 | async-start | bytes 7299072 | tf_op jit(solution)/shard_map/all_gather | solution.py:144
  133.7 1.1 copy-start.7
  138.3 1.1 copy-start.6
  141.2 1.5 copy-start.5
  147.9 0.9 copy-start.3
  157.9 6.8 %collective-permute-start.2 = (bf16[64,1,4,128]{0,3,2,1:T(8,128)(2,1)S(1)}, bf16[64,1,4,128]{0,3,2,1:T(8,128)(2,1)S(1)}, u32[]{:S(2)}, u32[]{:S(2)}) collective-permute-start(bf16[64,1,4,128]{0,3,2,1:T(8,128)(2,1)S(1)} %slice.614), channel_id=1, source_target_pairs={{1,0},{2,1},{3,2},{4,3},{5,4},{6,5},{7,6},{8,7},{9,8},{10,9},{11,1... | collective-permute-start | bytes 196616 | tf_op jit(solution)/shard_map/ppermute | solution.py:11
Sparse Core Ops, SparseCore 0:
  37.8 45.7 all-gather.2
  130.7 268.8 all-reduce.17
  402.8 93.0 all-gather.4
